TPU v7x, 32 devices: a whole 2x2x4 slice. The times are simulated.
32 devices in a mesh: seq: 8 (over z, x), tp: 4 (over y, core).
Axes of the slice: x: 2, y: 2, z: 4, core: 2. Of those that a mesh axis runs over, the one named last changes fastest.
Arguments:
- byte_states: bfloat16 [4096, 1024], P('seq'), may hold values from -6 to 6
- flags: int32 [4096], P('seq'), may hold values from 0 to 1, as said below
- stretch_owner: int32 [1024, 1], P('seq'), may hold values from 0 to 7; in each aligned block of 128 rows (0 to 127, 128 to 255, ...) at most 32 rows name the same one
- log_decay: float32 [4096, 16], P('seq', 'tp'), may hold values from -2 to 0, as said below
- w_x: bfloat16 [1024, 2048], P(None, 'tp'), may hold values from -0.1875 to 0.1875
- w_z: bfloat16 [1024, 2048], P(None, 'tp'), may hold values from -0.1875 to 0.1875
- w_bc: bfloat16 [1024, 256], replicated, may hold values from -0.1875 to 0.1875
- w_out: bfloat16 [2048, 1024], P('tp'), may hold values from -0.125 to 0.125
- pad_vector: bfloat16 [512], replicated, may hold values from -5 to 5
- w_q: bfloat16 [1536, 1536], P(None, 'tp'), may hold values from -8 to 8
- w_k: bfloat16 [1536, 1536], P(None, 'tp'), may hold values from -8 to 8
- w_v: bfloat16 [1536, 1536], P(None, 'tp'), may hold values from -0.15625 to 0.15625
- w_o: bfloat16 [1536, 1536], P('tp'), may hold values from -0.15625 to 0.15625
Outputs:
- enc_out: bfloat16 [4096, 1024], P('seq', 'tp')
- main_out: bfloat16 [2048, 1536], P('seq')
Inputs may be any that keep to these rules, and one draw needn't show every extreme that they name: `flags`: exactly 128 ones among each aligned block of 512 bytes. `stretch_owner`: in each aligned block of 128 stretches no owner is named more than 32 times. `log_decay`: negative.
All inputs are finite; a program needn't handle non-finite values.
Results may differ from a plain program's by a relative error of at most 0.015.
Values may be sent and summed in bfloat16 or wider, within the bound.
A program may use at most 128 MiB of HBM per device.

v0:
```python
import math
import jax
import jax.numpy as jnp
from jax import lax
from jax.sharding import PartitionSpec as P

HD = 128
BLOCK = 256
eps = 1e-05
highest = lax.Precision.HIGHEST
far_query = 536870912
far_key = 1073741824


def carried_in(shard, axis, combine, identity):
    peers, index = (lax.axis_size(axis), lax.axis_index(axis))
    everything = jax.tree.map(
        lambda part, kind: lax.all_gather(part.astype(kind), axis),
        shard,
        (jnp.bfloat16, jnp.bfloat16),
    )
    start = jax.tree.map(
        lambda part, zero: jnp.broadcast_to(jnp.asarray(zero, part.dtype), part.shape),
        shard,
        identity,
    )

    def carried_step(k, before):
        reached = k < index
        new = combine(
            before, jax.tree.map(lambda part, own: part[k].astype(own.dtype), everything, shard)
        )
        return jax.tree.map(lambda a, b: jnp.where(reached, a, b), new, before)

    return lax.fori_loop(0, peers, carried_step, start)


def shortened(shard):

    def short(part):
        return part.astype(jnp.bfloat16) if part.dtype == jnp.float32 else part

    return jax.tree.map(short, shard)


def rms_rows(values):
    wide = values.astype(jnp.float32)
    return wide * lax.rsqrt(jnp.mean(wide * wide, axis=-1, keepdims=True) + eps)


def ssd_blocks(xh, bmat, cmat, decay, start_state):
    rows, heads, width_p = xh.shape
    nblk = rows // BLOCK

    def advance(state, block):
        x_blk, b_blk, c_blk, a_blk = block
        cum = jnp.cumsum(a_blk, axis=0)
        later = lax.broadcasted_iota(jnp.int32, (BLOCK, BLOCK), 0)
        earlier = lax.broadcasted_iota(jnp.int32, (BLOCK, BLOCK), 1)
        causal = (later >= earlier)[:, :, None]
        spans = jnp.where(causal, cum[:, None, :] - cum[None, :, :], -1e30)
        intersection = jnp.dot(c_blk, b_blk.T, preferred_element_type=jnp.float32)
        mixing = intersection[:, :, None] * jnp.exp(spans)
        x_wide = x_blk.astype(jnp.float32)
        inside = jnp.einsum("tsh,shp->thp", mixing, x_wide, precision=highest)
        carried = (
            jnp.einsum("tn,hnp->thp", c_blk.astype(jnp.float32), state, precision=highest)
            * jnp.exp(cum)[:, :, None]
        )
        tail = jnp.exp(cum[-1][None, :] - cum)
        fresh = jnp.einsum(
            "sh,sn,shp->hnp", tail, b_blk.astype(jnp.float32), x_wide, precision=highest
        )
        new_state = state * jnp.exp(cum[-1])[:, None, None] + fresh
        return (new_state, inside + carried)

    blocks = (
        xh.reshape(nblk, BLOCK, heads, width_p),
        bmat.reshape(nblk, BLOCK, -1),
        cmat.reshape(nblk, BLOCK, -1),
        decay.reshape(nblk, BLOCK, heads),
    )
    final, outs = lax.scan(advance, start_state, blocks)
    return (outs.reshape(rows, heads, width_p), final)


def link_states(earlier, later):
    return (earlier[0] + later[0], earlier[1] * jnp.exp(later[0])[..., None, None] + later[1])


def attend_block(carry, queries, query_pos, key_blk, value_blk, key_pos, scale):
    best, total, accum = carry
    scores = (
        jnp.einsum("qhd,khd->hqk", queries, key_blk, preferred_element_type=jnp.float32) * scale
    )
    allowed = key_pos[None, None, :] <= query_pos[None, :, None]
    scores = jnp.where(allowed, scores, -1e30)
    new_best = jnp.maximum(best, jnp.max(scores, axis=2))
    shrink = jnp.exp(best - new_best)
    expo = jnp.where(allowed, jnp.exp(scores - new_best[:, :, None]), 0.0)
    total = total * shrink + jnp.sum(expo, axis=2)
    accum = accum * jnp.transpose(shrink)[:, :, None] + jnp.einsum(
        "hqk,khd->qhd", expo.astype(jnp.bfloat16), value_blk, preferred_element_type=jnp.float32
    )
    return (new_best, total, accum)


def on_device(
    byte_states,
    flags,
    stretch_owner,
    log_decay,
    w_x,
    w_z,
    w_bc,
    w_out,
    pad_vector,
    w_q,
    w_k,
    w_v,
    w_o,
):
    rows, width = byte_states.shape
    heads_here = log_decay.shape[1]
    head_p = w_x.shape[1] // heads_here
    state_n = w_bc.shape[1] // 2
    ranks = lax.axis_size("seq")
    split_tp = lax.axis_size("tp")
    normed = rms_rows(byte_states).astype(jnp.bfloat16)
    xs = jnp.dot(normed, w_x, preferred_element_type=jnp.float32).astype(jnp.bfloat16)
    zgate = jnp.dot(normed, w_z, preferred_element_type=jnp.float32)
    projected = jnp.dot(normed, w_bc, preferred_element_type=jnp.float32).astype(jnp.bfloat16)
    bmat = projected[:, :state_n]
    cmat = projected[:, state_n:]
    start_state = jnp.zeros((heads_here, state_n, head_p), jnp.float32)
    local_mixed, final = ssd_blocks(
        xs.reshape(rows, heads_here, head_p), bmat, cmat, log_decay, start_state
    )
    running = jnp.cumsum(log_decay, axis=0)
    identity = (jnp.zeros((heads_here,), jnp.float32), jnp.zeros_like(final))
    carried = carried_in((running[-1], final), "seq", link_states, identity)
    incoming = carried[1]
    mixed = (
        local_mixed
        + jnp.einsum("tn,hnp->thp", cmat.astype(jnp.float32), incoming, precision=highest)
        * jnp.exp(running)[:, :, None]
    )
    gated = mixed * jax.nn.silu(zgate).reshape(rows, heads_here, head_p)
    scaled = gated * lax.rsqrt(jnp.mean(gated * gated, axis=2, keepdims=True) + eps)
    scaled = scaled.reshape(rows, heads_here * head_p).astype(jnp.bfloat16)
    partial_enc = jnp.dot(scaled, w_out, preferred_element_type=jnp.float32)
    quarter = width // split_tp
    column_start = lax.axis_index("tp") * quarter
    stretches_here = stretch_owner.shape[0]
    flag_rank = jnp.cumsum(flags) - 1
    stretch_ids = lax.broadcasted_iota(jnp.int32, (stretches_here, rows), 0)
    picker = ((flag_rank[None, :] == stretch_ids) & (flags[None, :] == 1)).astype(jnp.bfloat16)
    summed = lax.psum(partial_enc.astype(jnp.bfloat16), "tp").astype(jnp.float32)
    encoded = (byte_states.astype(jnp.float32) + summed).astype(jnp.bfloat16)
    enc_out = lax.dynamic_slice_in_dim(encoded, column_start, quarter, 1)
    stretch_rows = jnp.dot(picker, encoded, preferred_element_type=jnp.float32).astype(jnp.bfloat16)
    cap = max(2, 2 * stretches_here // ranks)
    slots = ranks * cap
    owners = stretch_owner[:, 0]
    owner_hot = (
        owners[:, None] == lax.broadcasted_iota(jnp.int32, (stretches_here, ranks), 1)
    ).astype(jnp.int32)
    before = jnp.cumsum(owner_hot, axis=0) - owner_hot
    order = jnp.sum(before * owner_hot, axis=1)
    slot = owners * cap + order
    slot_ids = lax.broadcasted_iota(jnp.int32, (slots, stretches_here), 0)
    placed = slot_ids == slot[None, :]
    anchor = lax.axis_index("seq") * stretches_here + lax.broadcasted_iota(
        jnp.int32, (stretches_here,), 0
    )
    send_pos = jnp.where(
        jnp.any(placed, axis=1), jnp.sum(jnp.where(placed, anchor[None, :], 0), axis=1), -1
    )
    send_rows = jnp.dot(
        placed.astype(jnp.bfloat16), stretch_rows, preferred_element_type=jnp.float32
    ).astype(jnp.bfloat16)
    got_rows, got_pos = (
        lax.all_to_all(
            send_rows.reshape(ranks, cap, width), "seq", split_axis=0, concat_axis=0, tiled=True
        ),
        lax.all_to_all(
            send_pos.reshape(ranks, cap), "seq", split_axis=0, concat_axis=0, tiled=True
        ),
    )
    got_rows = got_rows.reshape(slots, width)
    got_pos = got_pos.reshape(slots)
    valid = got_pos >= 0
    padding = jnp.where(valid[:, None], pad_vector[None, :], jnp.zeros((), jnp.bfloat16))
    stream = jnp.concatenate([got_rows, padding], axis=1)
    stream_norm = rms_rows(stream).astype(jnp.bfloat16)
    heads_main = w_q.shape[1] // HD
    scale = 1.0 / math.sqrt(HD)
    queries = (
        jnp.dot(stream_norm, w_q, preferred_element_type=jnp.float32)
        .astype(jnp.bfloat16)
        .reshape(slots, heads_main, HD)
    )
    query_pos = jnp.where(valid, got_pos, far_query)
    start_carry = (
        jnp.full((heads_main, slots), -1e30, jnp.float32),
        jnp.zeros((heads_main, slots), jnp.float32),
        jnp.zeros((slots, heads_main, HD), jnp.float32),
    )
    keys_here = (
        jnp.dot(stream_norm, w_k, preferred_element_type=jnp.float32)
        .astype(jnp.bfloat16)
        .reshape(slots, heads_main, HD)
    )
    values_here = (
        jnp.dot(stream_norm, w_v, preferred_element_type=jnp.float32)
        .astype(jnp.bfloat16)
        .reshape(slots, heads_main, HD)
    )
    key_pos_here = jnp.where(valid, got_pos, far_key)
    key_rows = lax.all_gather(keys_here, "seq", axis=0, tiled=True)
    count = key_rows.shape[0]
    size = math.gcd(count, 512)
    nblk = count // size

    def fold_step(state, block):
        return (attend_block(state, queries, query_pos, block[0], block[1], block[2], scale), None)

    blocks = (
        key_rows.reshape(nblk, size, heads_main, HD),
        lax.all_gather(values_here, "seq", axis=0, tiled=True).reshape(nblk, size, heads_main, HD),
        lax.all_gather(shortened(key_pos_here), "seq", axis=0, tiled=True).reshape(nblk, size),
    )
    best, total, accum = lax.scan(fold_step, start_carry, blocks)[0]
    attended = (
        (accum / jnp.transpose(total)[:, :, None])
        .astype(jnp.bfloat16)
        .reshape(slots, heads_main * HD)
    )
    summed_main = lax.psum(
        jnp.dot(attended, w_o, preferred_element_type=jnp.float32).astype(jnp.bfloat16), "tp"
    ).astype(jnp.float32)
    main_out = jnp.where(valid[:, None], stream.astype(jnp.float32) + summed_main, 0.0).astype(
        jnp.bfloat16
    )
    return (enc_out, main_out)


def solution(mesh):
    placed = (
        P("seq", None),
        P("seq"),
        P("seq", None),
        P("seq", "tp"),
        P(None, "tp"),
        P(None, "tp"),
        P(),
        P("tp", None),
        P(),
        P(None, "tp"),
        P(None, "tp"),
        P(None, "tp"),
        P("tp", None),
    )
    return jax.shard_map(
        on_device,
        mesh=mesh,
        in_specs=placed,
        out_specs=(P("seq", "tp"), P("seq", None)),
        check_vma=False,
    )
```

profile of v0, /device:TPU:0, one launch (start us, length us, event | category | flops | bytes accessed | tf_op | source)
XLA Modules:
  0.0 318.6 jit_solution(18168973310382984664)
XLA Ops:
  7.2 1.6 fusion.45
  8.9 2.0 convolution_convert_fusion.4
  11.6 0.7 convolution_convert_fusion.3
  12.5 32.7 %while.42 = (s32[]{:T(128)}, f32[4,128,128]{2,1,0:T(8,128)S(1)}, f32[2,256,4,128]{1,0,3,2:T(2,128)}, f32[2,256,4]{1,2,0:T(4,128)S(1)}, bf16[2,256,128]{2,1,0:T(8...) while((s32[]{:T(128)}, f32[4,128,128]{2,1,0:T(8,128)S(1)}, ...), condition=%wide.region_4.5_spmd.clone, body=%wide.region_1.4_spmd.clone.sunk | while | flops 823755776 | bytes 7013988 | solution.py:83
  12.5 1.2 reduce-window.39
  15.8 1.0 fusion.114
  17.3 11.5 %dynamic_update_slice.6 = f32[2,256,4,128]{1,0,3,2:T(2,128)} dynamic-update-slice(f32[2,256,4,128]{1,0,3,2:T(2,128)} %get-tuple-element.594, f32[1,256,4,128]{1,0,3,2:T(1,128)S(1)} %copy.191, s32[]{:T(128)S(6)} %copy.196, s32[]{:T(128)} %constant.107.clone.1..sunk, s32[]{:T(128)} %constant.107.clone.1..sunk, s32[]{:T(128)} %constant.107.clone.1..sunk) | dynamic-update-slice | bytes 1048580 | tf_op jit(solution)/shard_map/while/body/jit(dynamic_update_index_in_dim)/dynamic_update_slice | solution.py:83
  28.9 1.2 reduce-window.39
  32.2 1.0 fusion.114
  33.7 11.5 %dynamic_update_slice.6 = f32[2,256,4,128]{1,0,3,2:T(2,128)} dynamic-update-slice(f32[2,256,4,128]{1,0,3,2:T(2,128)} %get-tuple-element.594, f32[1,256,4,128]{1,0,3,2:T(1,128)S(1)} %copy.191, s32[]{:T(128)S(6)} %copy.196, s32[]{:T(128)} %constant.107.clone.1..sunk, s32[]{:T(128)} %constant.107.clone.1..sunk, s32[]{:T(128)} %constant.107.clone.1..sunk) | dynamic-update-slice | bytes 1048580 | tf_op jit(solution)/shard_map/while/body/jit(dynamic_update_index_in_dim)/dynamic_update_slice | solution.py:83
  46.0 1.2 reduce-window.23
  49.6 7.3 %all-to-all-start = ((s32[8,1,32]{2,1,0:T(1,128)}), s32[8,1,32]{2,1,0:T(1,128)}, u32[]{:S(2)}, u32[]{:S(2)}) async-start(s32[8,1,32]{2,1,0:T(1,128)} %select_n.72), calls=%async_computation | async-start | bytes 8192 | tf_op jit(solution)/shard_map/all_to_all | solution.py:186
  56.9 21.2 %all-gather.1 = bf16[8,1,4]{2,1,0:T(2,128)(2,1)} all-gather(bf16[1,1,4]{2,1,0:T(2,128)(2,1)S(1)} %slice_bitcast_fusion), channel_id=1, replica_groups=mesh['seq'=8,'tp'=4] {'seq'}, dimensions={0}, use_global_device_ids=true | all-gather | bytes 72 | tf_op jit(solution)/shard_map/all_gather | solution.py:18
  78.1 2.1 reshape.237
  80.2 0.8 copy.137
  81.6 1.0 reduce-window.27
  83.3 3.2 %divide_multiply_fusion = f32[512,512]{0,1:T(8,128)} fusion(bf16[1024,512]{1,0:T(8,128)(2,1)} %param.24, bf16[512,1024]{1,0:T(8,128)(2,1)S(1)} %copy-done.5, f32[512]{0:T(512)} %copy-done.16), kind=kOutput, calls=%fused_computation.92 | convolution fusion | flops 539492352 | bytes 3147776 | tf_op jit(solution)/shard_map/dot_general | solution.py:131
  86.6 2.7 all-gather.11.cloned.1.call-done
  89.2 13.7 %while.43 = (s32[]{:T(128)}, f32[4,128,128]{2,1,0:T(8,128)S(1)}, s32[]{:T(128)}, bf16[8,4]{1,0:T(8,128)(2,1)}, bf16[8,4,128,128]{3,2,1,0:T(8,128)(2,1)}, /*index=5*/s32[]{:T(128)}, s32[]{:T(128)}) while((s32[]{:T(128)}, f32[4,128,128]{2,1,0:T(8,128)S(1)}, s32[]{:T(128)}, bf16[8,4]{1,0:T(8,128)(2,1)}, ...), condition=%wide.region_8.9_spmd.clone, body=%wide.region_7.8_spmd.clone.sunk | while | flops 327688 | bytes 655513 | solution.py:35
  89.9 1.0 fusion.115
  90.9 0.7 exponential_bitcast_fusion.3
  91.6 1.0 fusion.115
  92.6 0.7 exponential_bitcast_fusion.3
  93.3 1.0 fusion.115
  94.4 0.7 exponential_bitcast_fusion.3
  95.0 1.0 fusion.115
  96.1 0.7 exponential_bitcast_fusion.3
  96.7 1.0 fusion.115
  98.5 1.0 fusion.115
  100.2 1.0 fusion.115
  101.9 1.0 fusion.115
  102.9 0.8 copy.139
  103.7 1.7 fusion.62
  106.0 1.1 copy-done.19
  107.1 1.8 convolution_convert_fusion.1
  109.1 34.9 %all-reduce.3.cloned.1.call-done = bf16[512,1024]{1,0:T(8,128)(2,1)} async-done(((bf16[512,1024]{1,0:T(8,128)(2,1)}), bf16[512,1024]{1,0:T(8,128)(2,1)}) %all-reduce.3.cloned.1.call-update) | async-done | bytes 1048592 | tf_op jit(solution)/shard_map/psum | solution.py:158
  144.0 1.6 fusion.47
  145.7 1.3 convolution_convert_fusion.2
  147.0 5.5 %all-to-all-start.1 = ((bf16[8,32,1024]{2,1,0:T(8,128)(2,1)}), bf16[8,32,1024]{2,1,0:T(8,128)(2,1)S(1)}, u32[]{:S(2)}, u32[]{:S(2)}) async-start(bf16[8,32,1024]{2,1,0:T(8,128)(2,1)} %bitcast.182), calls=%async_computation.1 | async-start | bytes 1048576 | tf_op jit(solution)/shard_map/all_to_all | solution.py:183
  153.1 1.3 reduce.10
  154.6 11.8 %all-to-all-done.1 = bf16[8,32,1024]{2,1,0:T(8,128)(2,1)S(1)} async-done(((bf16[8,32,1024]{2,1,0:T(8,128)(2,1)}), bf16[8,32,1024]{2,1,0:T(8,128)(2,1)S(1)}, u32[]{:S(2)}, u32[]{:S(2)}) %all-to-all-start.1) | async-done | bytes 524320 | tf_op jit(solution)/shard_map/all_to_all | solution.py:183
  166.7 1.9 convolution_convert_fusion.8
  168.6 0.8 copy.140
  169.7 1.9 convolution_convert_fusion.6
  171.6 0.8 copy.143
  172.5 18.7 %all-gather.2 = s32[8,1,256]{2,1,0:T(1,128)S(1)} all-gather(s32[1,1,256]{2,1,0:T(1,128)S(1)} %bitcast.201), channel_id=1, replica_groups=mesh['seq'=8,'tp'=4] {'seq'}, dimensions={0}, use_global_device_ids=true | all-gather | bytes 9216 | tf_op jit(solution)/shard_map/all_gather | solution.py:231
  191.2 1.9 convolution_convert_fusion.7
  193.4 19.5 %all-gather.7.cloned.1.call-done = bf16[2048,3,128]{0,2,1:T(8,128)(2,1)} async-done(((bf16[256,3,128]{0,2,1:T(8,128)(2,1)}), bf16[2048,3,128]{0,2,1:T(8,128)(2,1)}) %all-gather.7.cloned.1.call-update) | async-done | bytes 1572880 | tf_op jit(solution)/shard_map/all_gather | solution.py:220
  213.0 2.6 copy.141
  215.6 42.5 %all-gather.9.cloned.1.call-done = bf16[2048,3,128]{0,2,1:T(8,128)(2,1)} async-done(((bf16[256,3,128]{0,2,1:T(8,128)(2,1)}), bf16[2048,3,128]{0,2,1:T(8,128)(2,1)}) %all-gather.9.cloned.1.call-update) | async-done | bytes 1572880 | tf_op jit(solution)/shard_map/all_gather | solution.py:230
  258.1 2.6 copy.144
  260.7 14.2 %while.44 = (s32[]{:T(128)}, f32[3,256]{1,0:T(4,128)S(1)}, f32[3,256]{1,0:T(4,128)S(1)}, f32[256,3,128]{0,2,1:T(8,128)S(1)}, s32[4,512]{1,0:T(4,128)S(1)}, /*ind...) while((s32[]{:T(128)}, f32[3,256]{1,0:T(4,128)S(1)}, ...), condition=%wide.region_21.22_spmd.clone, body=%wide.region_18.21_spmd.clone.sunk | while | flops 205296128 | bytes 7068813 | solution.py:233
  260.8 1.4 fusion.119
  262.6 1.6 fusion.123
  264.4 1.4 fusion.119
  266.2 1.6 fusion.123
  267.9 1.4 fusion.119
  269.7 1.6 fusion.123
  271.5 1.4 fusion.119
  273.2 1.6 fusion.123
  274.9 1.5 convolution_convert_fusion
  276.4 1.7 constant_dynamic-slice_fusion.4
  278.1 31.7 %all-reduce.5.cloned.1.call-done = bf16[256,1536]{1,0:T(8,128)(2,1)} async-done(((bf16[256,1536]{1,0:T(8,128)(2,1)}), bf16[256,1536]{1,0:T(8,128)(2,1)}) %all-reduce.5.cloned.1.call-update) | async-done | bytes 786448 | tf_op jit(solution)/shard_map/psum | solution.py:239
  309.8 2.3 fusion.51
  (167 shorter events, 17.6 us)
Async XLA Ops:
  7.2 267.7 %copy-start = (bf16[384,1536]{1,0:T(8,128)(2,1)S(1)}, bf16[384,1536]{1,0:T(8,128)(2,1)}, u32[]{:S(2)}) copy-start(bf16[384,1536]{1,0:T(8,128)(2,1)} %param.31) | copy-start | bytes 3538948
  7.2 82.0 %all-gather.11.cloned.1.call-start = ((), (), s32[]{:S(2)}) async-start(), calls=%async_computation.6 | async-start | bytes 1179648 | tf_op jit(solution)/shard_map/all_gather | solution.py:18
  8.8 2.7 copy-start.4
  8.8 2.7 copy-start.18
  8.9 3.5 %copy-start.16 = (f32[512]{0:T(512)}, f32[512]{0:T(512)S(1)}, u32[]{:S(2)}) copy-start(f32[512]{0:T(512)S(1)} %add_rsqrt_fusion.1) | copy-start | bytes 6148
  10.9 0.7 copy-start.9
  11.6 0.9 copy-start.10
  12.5 35.3 %copy-start.13 = (s32[128,1]{0,1:T(1,128)S(1)}, s32[128,1]{0,1:T(1,128)}, u32[]{:S(2)}) copy-start(s32[128,1]{0,1:T(1,128)} %param.21) | copy-start | bytes 1540
  45.2 38.1 %copy-start.5 = (bf16[512,1024]{1,0:T(8,128)(2,1)S(1)}, bf16[512,1024]{1,0:T(8,128)(2,1)}, u32[]{:S(2)}) copy-start(bf16[512,1024]{1,0:T(8,128)(2,1)} %param.19) | copy-start | bytes 3145732
  48.3 0.5 copy-start.14
  49.6 97.4 %all-to-all-start = ((s32[8,1,32]{2,1,0:T(1,128)}), s32[8,1,32]{2,1,0:T(1,128)}, u32[]{:S(2)}, u32[]{:S(2)}) async-start(s32[8,1,32]{2,1,0:T(1,128)} %select_n.72), calls=%async_computation | async-start | bytes 8192 | tf_op jit(solution)/shard_map/all_to_all | solution.py:186
  56.9 87.2 %all-reduce.3.cloned.1.call-start = ((), (), s32[]{:S(2)}) async-start(), calls=%async_computation.2 | async-start | bytes 2097152 | tf_op jit(solution)/shard_map/psum | solution.py:158
  103.7 1.7 copy-start.8
  105.9 1.2 copy-start.19
  107.1 1.8 copy-start.11
  107.1 1.9 copy-start.12
  109.1 36.6 %copy-start.15 = (s32[128]{0:T(128)S(1)}, s32[128]{0:T(128)}, u32[]{:S(2)}) copy-start(s32[128]{0:T(128)} %copy-done.14) | copy-start | bytes 1540
  145.7 21.0 %copy-start.1 = (bf16[512,1024]{1,0:T(8,128)(2,1)}, bf16[512,1024]{1,0:T(8,128)(2,1)S(1)}, u32[]{:S(2)}) copy-start(bf16[512,1024]{1,0:T(8,128)(2,1)S(1)} %fusion.47) | copy-start | bytes 3145732
  145.7 8.8 %copy-start.17 = (bf16[512]{0:T(512)(128)(2,1)S(1)}, bf16[512]{0:T(512)(128)(2,1)}, u32[]{:S(2)}) copy-start(bf16[512]{0:T(512)(128)(2,1)} %param.27) | copy-start | bytes 3076
  147.0 19.5 %all-to-all-start.1 = ((bf16[8,32,1024]{2,1,0:T(8,128)(2,1)}), bf16[8,32,1024]{2,1,0:T(8,128)(2,1)S(1)}, u32[]{:S(2)}, u32[]{:S(2)}) async-start(bf16[8,32,1024]{2,1,0:T(8,128)(2,1)} %bitcast.182), calls=%async_computation.1 | async-start | bytes 1048576 | tf_op jit(solution)/shard_map/all_to_all | solution.py:183
  152.5 60.5 %all-gather.7.cloned.1.call-start = ((), (), s32[]{:S(2)}) async-start(), calls=%async_computation.3 | async-start | bytes 1769472 | tf_op jit(solution)/shard_map/all_gather | solution.py:220
  154.6 36.6 %copy-start.6 = (bf16[256,512]{1,0:T(8,128)(2,1)}, bf16[256,512]{1,0:T(8,128)(2,1)S(1)}, u32[]{:S(2)}) copy-start(bf16[256,512]{1,0:T(8,128)(2,1)S(1)} %broadcast_select_fusion) | copy-start | bytes 786436
  166.5 24.8 %copy-start.2 = (bf16[8,32,1024]{2,1,0:T(8,128)(2,1)}, bf16[8,32,1024]{2,1,0:T(8,128)(2,1)S(1)}, u32[]{:S(2)}) copy-start(bf16[8,32,1024]{2,1,0:T(8,128)(2,1)S(1)} %all-to-all-done.1) | copy-start | bytes 1572868
  169.5 88.6 %all-gather.9.cloned.1.call-start = ((), (), s32[]{:S(2)}) async-start(), calls=%async_computation.4 | async-start | bytes 1769472 | tf_op jit(solution)/shard_map/all_gather | solution.py:230
  172.4 137.4 %all-reduce.5.cloned.1.call-start = ((), (), s32[]{:S(2)}) async-start(), calls=%async_computation.5 | async-start | bytes 1572864 | tf_op jit(solution)/shard_map/psum | solution.py:239
  274.9 34.9 %copy-start.3 = (bf16[8,32,1024]{2,1,0:T(8,128)(2,1)S(1)}, bf16[8,32,1024]{2,1,0:T(8,128)(2,1)}, u32[]{:S(2)}) copy-start(bf16[8,32,1024]{2,1,0:T(8,128)(2,1)} %copy-done.2) | copy-start | bytes 1572868
  274.9 34.9 %copy-start.7 = (bf16[256,512]{1,0:T(8,128)(2,1)S(1)}, bf16[256,512]{1,0:T(8,128)(2,1)}, u32[]{:S(2)}) copy-start(bf16[256,512]{1,0:T(8,128)(2,1)} %copy-done.6) | copy-start | bytes 786436
Sparse Core Ops, SparseCore 0:
  46.1 43.1 all-gather.10
  109.0 34.9 all-reduce.2
  169.6 43.3 all-gather.6
  215.4 42.5 all-gather.8
  276.5 33.2 all-reduce.4
where the time goes:
time: 321 us; the launch traced here: 319 us
  waiting for transfers between devices  143 us (45%)
  local copies, waits for them, and re-layouts  43 us (13%)
  blocking collectives  39.8 us (12%)
  matrix products  33.9 us (11%)
  other arithmetic  30.7 us (10%)
  between operations  14.2 us (4%)
  starting transfers between devices  13.2 us (4%)
    all_gather x1, waiting for transfers between devices, on_device(): lax.all_gather(values_here, 'seq', axis=0, tiled=True)  42.5 us
    psum x1, waiting for transfers between devices, on_device(): lax.psum(partial_enc.astype(jnp.bfloat16), 'tp').astype(jnp.float32)  34.9 us
    psum x1, waiting for transfers between devices, on_device(): lax.psum(jnp.dot(attended, w_o, preferred_element_type=jnp.float32).astyp...  31.7 us
    dynamic_update_slice x4, local copies, waits for them, and re-layouts, ssd_blocks(): final, outs = lax.scan(advance, start_state, blocks)  24.1 us
    all_gather x1, blocking collectives, carried_in(): lax.all_gather(part.astype(kind), axis)  21.2 us
    all_gather x1, waiting for transfers between devices, on_device(): key_rows = lax.all_gather(keys_here, 'seq', axis=0, tiled=True)  19.5 us
    all_gather x1, blocking collectives, on_device(): lax.all_gather(shortened(key_pos_here), 'seq', axis=0, tiled=True)  18.7 us
    all_to_all x1, waiting for transfers between devices, on_device(): lax.all_to_all(send_rows.reshape(ranks, cap, width), 'seq', split_axis=0,...  11.8 us
  transfers between devices with their start and end apart: 7, of which 6 were waited for; matrix products, arithmetic and copies ran while one was open for 14% of the time, Pallas kernels for 0%

commit v1 on v0

--- a/solution.py
+++ b/solution.py
@@ -10,6 +10,12 @@
 highest = lax.Precision.HIGHEST
 far_query = 536870912
 far_key = 1073741824
+
+
+def laid_out(blocks, dim):
+    blocks = jnp.moveaxis(blocks, 0, dim)
+    lengths = blocks.shape
+    return blocks.reshape(*lengths[:dim], lengths[dim] * lengths[dim + 1], *lengths[dim + 2 :])
 
 
 def carried_in(shard, axis, combine, identity):
@@ -217,7 +223,19 @@
         .reshape(slots, heads_main, HD)
     )
     key_pos_here = jnp.where(valid, got_pos, far_key)
-    key_rows = lax.all_gather(keys_here, "seq", axis=0, tiled=True)
+    devices = lax.axis_size("seq")
+    pairs = [(i, (i + 1) % devices) for i in range(devices)]
+    back = [(b_2, a_2) for a_2, b_2 in pairs]
+    lower, upper = ([], [])
+    for step in range(devices - 1):
+        if step % 2 == 0:
+            lower.append(lax.ppermute(lower[-1] if lower else keys_here, "seq", pairs))
+        else:
+            upper.append(lax.ppermute(upper[-1] if upper else keys_here, "seq", back))
+    parts = jnp.stack([*lower[::-1], keys_here, *upper])
+    shift = lax.axis_index("seq") - len(lower)
+    parts = parts[(jnp.arange(devices) - shift) % devices]
+    key_rows = laid_out(parts, 0)
     count = key_rows.shape[0]
     size = math.gcd(count, 512)
     nblk = count // size

time: 321 us -> 301 us (0.938)
  waiting for transfers between devices: 143 us -> 103 us
  local copies, waits for them, and re-layouts: 43 us -> 51.6 us
  starting transfers between devices: 13.2 us -> 21.5 us
    all_gather x1, waiting for transfers between devices: 42.5 us -> 0.01 us  [on_device(): lax.all_gather(values_here, 'seq', axis=0, tiled=True)]
    all_gather x1 -> x0, waiting for transfers between devices: 19.5 us -> none  [on_device(): key_rows = lax.all_gather(keys_here, 'seq', axis=0, tiled=True)]
    ppermute x0 -> x7, waiting for transfers between devices: none -> 18.7 us  [the longest x4 12.7 us: on_device(): lower.append(lax.ppermute(lower[-1] if lower else keys_here, 'seq', pairs))]
    ppermute x0 -> x7, starting transfers between devices: none -> 8.34 us  [the longest x3 4.99 us: on_device(): upper.append(lax.ppermute(upper[-1] if upper else keys_here, 'seq', back))]
    unnamed x44 -> x51, local copies, waits for them, and re-layouts: 3.06 us -> 9.68 us
    gather x0 -> x2, local copies, waits for them, and re-layouts: none -> 3.63 us  [on_device(): parts = parts[(jnp.arange(devices) - shift) % devices]]
  transfers between devices with their start and end apart: 7 -> 13, of which waited for: 6 -> 7; matrix products, arithmetic and copies ran while one was open for 14% -> 18% of each run, Pallas kernels for 0% -> 0%
where the time goes in v1:
time: 301 us; the launch traced here: 298 us
  waiting for transfers between devices  103 us (34%)
  local copies, waits for them, and re-layouts  51.6 us (17%)
  blocking collectives  42.3 us (14%)
  matrix products  34.6 us (11%)
  other arithmetic  30.7 us (10%)
  starting transfers between devices  21.5 us (7%)
  between operations  14.2 us (5%)
    psum x1, waiting for transfers between devices, on_device(): lax.psum(partial_enc.astype(jnp.bfloat16), 'tp').astype(jnp.float32)  34.8 us
    psum x1, waiting for transfers between devices, on_device(): lax.psum(jnp.dot(attended, w_o, preferred_element_type=jnp.float32).astyp...  34.8 us
    dynamic_update_slice x4, local copies, waits for them, and re-layouts, ssd_blocks(): final, outs = lax.scan(advance, start_state, blocks)  24.1 us
    all_gather x1, blocking collectives, carried_in(): lax.all_gather(part.astype(kind), axis)  21.2 us
    all_gather x1, blocking collectives, on_device(): lax.all_gather(shortened(key_pos_here), 'seq', axis=0, tiled=True)  21.1 us
    ppermute x4, waiting for transfers between devices, on_device(): lower.append(lax.ppermute(lower[-1] if lower else keys_here, 'seq', pairs))  12.7 us
    all_to_all x1, waiting for transfers between devices, on_device(): lax.all_to_all(send_rows.reshape(ranks, cap, width), 'seq', split_axis=0,...  11.8 us
    unnamed x51, local copies, waits for them, and re-layouts  9.68 us
  transfers between devices with their start and end apart: 13, of which 7 were waited for; matrix products, arithmetic and copies ran while one was open for 18% of the time, Pallas kernels for 0%

profile of v1, /device:TPU:0, one launch (start us, length us, event | category | flops | bytes accessed | tf_op | source)
XLA Modules:
  0.0 298.3 jit_solution(14633987886940390819)
XLA Ops:
  7.2 1.6 fusion.45
  8.9 2.0 convolution_convert_fusion.4
  12.5 32.7 %while.42 = (s32[]{:T(128)}, f32[4,128,128]{2,1,0:T(8,128)S(1)}, f32[2,256,4,128]{1,0,3,2:T(2,128)}, f32[2,256,4]{1,2,0:T(4,128)S(1)}, bf16[2,256,128]{2,1,0:T(8...) while((s32[]{:T(128)}, f32[4,128,128]{2,1,0:T(8,128)S(1)}, ...), condition=%wide.region_4.5_spmd.clone, body=%wide.region_1.4_spmd.clone.sunk | while | flops 823755776 | bytes 7013988 | solution.py:89
  12.5 1.2 reduce-window.39
  15.8 1.0 fusion.116
  17.3 11.5 %dynamic_update_slice.6 = f32[2,256,4,128]{1,0,3,2:T(2,128)} dynamic-update-slice(f32[2,256,4,128]{1,0,3,2:T(2,128)} %get-tuple-element.594, f32[1,256,4,128]{1,0,3,2:T(1,128)S(1)} %copy.196, s32[]{:T(128)S(6)} %copy.201, s32[]{:T(128)} %constant.123.clone.1..sunk, s32[]{:T(128)} %constant.123.clone.1..sunk, s32[]{:T(128)} %constant.123.clone.1..sunk) | dynamic-update-slice | bytes 1048580 | tf_op jit(solution)/shard_map/while/body/jit(dynamic_update_index_in_dim)/dynamic_update_slice | solution.py:89
  28.9 1.2 reduce-window.39
  32.2 1.0 fusion.116
  33.7 11.5 %dynamic_update_slice.6 = f32[2,256,4,128]{1,0,3,2:T(2,128)} dynamic-update-slice(f32[2,256,4,128]{1,0,3,2:T(2,128)} %get-tuple-element.594, f32[1,256,4,128]{1,0,3,2:T(1,128)S(1)} %copy.196, s32[]{:T(128)S(6)} %copy.201, s32[]{:T(128)} %constant.123.clone.1..sunk, s32[]{:T(128)} %constant.123.clone.1..sunk, s32[]{:T(128)} %constant.123.clone.1..sunk) | dynamic-update-slice | bytes 1048580 | tf_op jit(solution)/shard_map/while/body/jit(dynamic_update_index_in_dim)/dynamic_update_slice | solution.py:89
  46.0 1.2 reduce-window.23
  49.6 7.3 %all-to-all-start = ((s32[8,1,32]{2,1,0:T(1,128)}), s32[8,1,32]{2,1,0:T(1,128)}, u32[]{:S(2)}, u32[]{:S(2)}) async-start(s32[8,1,32]{2,1,0:T(1,128)} %select_n.96), calls=%async_computation | async-start | bytes 8192 | tf_op jit(solution)/shard_map/all_to_all | solution.py:192
  56.9 21.2 %all-gather.1 = bf16[8,1,4]{2,1,0:T(2,128)(2,1)} all-gather(bf16[1,1,4]{2,1,0:T(2,128)(2,1)S(1)} %slice_bitcast_fusion), channel_id=1, replica_groups=mesh['seq'=8,'tp'=4] {'seq'}, dimensions={0}, use_global_device_ids=true | all-gather | bytes 72 | tf_op jit(solution)/shard_map/all_gather | solution.py:24
  78.1 2.1 reshape.283
  81.6 1.0 reduce-window.27
  83.3 3.2 %divide_multiply_fusion = f32[512,512]{0,1:T(8,128)} fusion(bf16[1024,512]{1,0:T(8,128)(2,1)} %param.24, bf16[512,1024]{1,0:T(8,128)(2,1)S(1)} %copy-done.5, f32[512]{0:T(512)} %copy-done.16), kind=kOutput, calls=%fused_computation.93 | convolution fusion | flops 539492352 | bytes 3147776 | tf_op jit(solution)/shard_map/dot_general | solution.py:137
  86.5 2.8 all-gather.8.cloned.1.call-done
  89.3 13.7 %while.43 = (s32[]{:T(128)}, f32[4,128,128]{2,1,0:T(8,128)S(1)}, s32[]{:T(128)}, bf16[8,4]{1,0:T(8,128)(2,1)}, bf16[8,4,128,128]{3,2,1,0:T(8,128)(2,1)}, /*index=5*/s32[]{:T(128)}, s32[]{:T(128)}) while((s32[]{:T(128)}, f32[4,128,128]{2,1,0:T(8,128)S(1)}, s32[]{:T(128)}, bf16[8,4]{1,0:T(8,128)(2,1)}, ...), condition=%wide.region_8.9_spmd.clone, body=%wide.region_7.8_spmd.clone.sunk | while | flops 327688 | bytes 655513 | solution.py:41
  90.0 1.0 fusion.117
  91.7 1.0 fusion.117
  93.4 1.0 fusion.117
  95.1 1.0 fusion.117
  96.8 1.0 fusion.117
  98.6 1.0 fusion.117
  100.3 1.0 fusion.117
  102.0 1.0 fusion.117
  103.0 0.8 copy.143
  103.8 1.7 fusion.64
  106.1 1.1 copy-done.19
  107.2 1.8 convolution_convert_fusion.1
  109.2 34.8 %all-reduce.3.cloned.1.call-done = bf16[512,1024]{1,0:T(8,128)(2,1)} async-done(((bf16[512,1024]{1,0:T(8,128)(2,1)}), bf16[512,1024]{1,0:T(8,128)(2,1)}) %all-reduce.3.cloned.1.call-update) | async-done | bytes 1048592 | tf_op jit(solution)/shard_map/psum | solution.py:164
  144.0 1.6 fusion.47
  145.6 1.3 convolution_convert_fusion.2
  146.9 5.5 %all-to-all-start.1 = ((bf16[8,32,1024]{2,1,0:T(8,128)(2,1)}), bf16[8,32,1024]{2,1,0:T(8,128)(2,1)S(1)}, u32[]{:S(2)}, u32[]{:S(2)}) async-start(bf16[8,32,1024]{2,1,0:T(8,128)(2,1)} %bitcast.199), calls=%async_computation.1 | async-start | bytes 1048576 | tf_op jit(solution)/shard_map/all_to_all | solution.py:189
  153.0 1.3 reduce.10
  154.6 11.8 %all-to-all-done.1 = bf16[8,32,1024]{2,1,0:T(8,128)(2,1)S(1)} async-done(((bf16[8,32,1024]{2,1,0:T(8,128)(2,1)}), bf16[8,32,1024]{2,1,0:T(8,128)(2,1)S(1)}, u32[]{:S(2)}, u32[]{:S(2)}) %all-to-all-start.1) | async-done | bytes 524320 | tf_op jit(solution)/shard_map/all_to_all | solution.py:189
  166.6 1.9 convolution_convert_fusion.6
  169.6 1.9 convolution_convert_fusion.8
  171.7 1.5 collective-permute-start
  173.1 7.0 %collective-permute-done = bf16[256,3,128]{0,2,1:T(8,128)(2,1)S(1)} collective-permute-done((bf16[256,3,128]{0,2,1:T(8,128)(2,1)S(1)}, bf16[256,3,128]{0,2,1:T(8,128)(2,1)S(1)}, u32[]{:S(2)}, u32[]{:S(2)}) %collective-permute-start) | collective-permute-done | bytes 196640 | tf_op jit(solution)/shard_map/ppermute | solution.py:232
  180.2 4.8 %collective-permute-start.4 = (bf16[256,3,128]{0,2,1:T(8,128)(2,1)S(1)}, bf16[256,3,128]{0,2,1:T(8,128)(2,1)S(1)}, u32[]{:S(2)}, u32[]{:S(2)}) collective-permute-start(bf16[256,3,128]{0,2,1:T(8,128)(2,1)S(1)} %bitcast.203), channel_id=1, source_target_pairs={{4,0},{8,4},{12,8},{16,12},{20,16},{24,20},{28,24},{0,28},{5,1},{9... | collective-permute-start | bytes 589832 | tf_op jit(solution)/shard_map/ppermute | solution.py:234
  185.0 5.6 %collective-permute-done.1 = bf16[256,3,128]{0,2,1:T(8,128)(2,1)S(1)} collective-permute-done((bf16[256,3,128]{0,2,1:T(8,128)(2,1)S(1)}, bf16[256,3,128]{0,2,1:T(8,128)(2,1)S(1)}, u32[]{:S(2)}, u32[]{:S(2)}) %collective-permute-start.1) | collective-permute-done | bytes 196640 | tf_op jit(solution)/shard_map/ppermute | solution.py:232
  190.6 21.1 %all-gather.2 = s32[8,1,256]{2,1,0:T(1,128)S(1)} all-gather(s32[1,1,256]{2,1,0:T(1,128)S(1)} %bitcast.220), channel_id=1, replica_groups=mesh['seq'=8,'tp'=4] {'seq'}, dimensions={0}, use_global_device_ids=true | all-gather | bytes 9216 | tf_op jit(solution)/shard_map/all_gather | solution.py:249
  212.0 1.9 collective-permute-start.3
  213.9 2.6 convolution_convert_fusion.7
  216.4 1.1 copy.147
  217.7 6.0 %collective-permute-done.5 = bf16[256,3,128]{0,2,1:T(8,128)(2,1)} collective-permute-done((bf16[256,3,128]{0,2,1:T(8,128)(2,1)S(1)}, bf16[256,3,128]{0,2,1:T(8,128)(2,1)}, u32[]{:S(2)}, u32[]{:S(2)}) %collective-permute-start.5) | collective-permute-done | bytes 196640 | tf_op jit(solution)/shard_map/ppermute | solution.py:234
  223.7 1.6 bitcast_dynamic-update-slice_fusion.6
  228.7 1.6 bitcast_dynamic-update-slice_fusion.1
  231.0 2.1 gather_fusion
  233.1 1.6 copy.146
  234.7 2.6 copy.149
  237.3 14.2 %while.44 = (s32[]{:T(128)}, f32[3,256]{1,0:T(4,128)S(1)}, f32[3,256]{1,0:T(4,128)S(1)}, f32[256,3,128]{0,2,1:T(8,128)S(1)}, s32[4,512]{1,0:T(4,128)S(1)}, /*ind...) while((s32[]{:T(128)}, f32[3,256]{1,0:T(4,128)S(1)}, ...), condition=%wide.region_21.22_spmd.clone, body=%wide.region_18.21_spmd.clone.sunk | while | flops 205296128 | bytes 7068813 | solution.py:251
  237.4 1.4 fusion.121
  239.2 1.6 fusion.125
  241.0 1.4 fusion.121
  242.8 1.6 fusion.125
  244.5 1.4 fusion.121
  246.3 1.6 fusion.125
  248.1 1.4 fusion.121
  249.8 1.6 fusion.125
  251.5 1.5 convolution_convert_fusion
  253.0 1.7 constant_dynamic-slice_fusion.4
  254.7 34.8 %all-reduce.5.cloned.1.call-done = bf16[256,1536]{1,0:T(8,128)(2,1)} async-done(((bf16[256,1536]{1,0:T(8,128)(2,1)}), bf16[256,1536]{1,0:T(8,128)(2,1)}) %all-reduce.5.cloned.1.call-update) | async-done | bytes 786448 | tf_op jit(solution)/shard_map/psum | solution.py:257
  289.5 2.3 fusion.51
  (189 shorter events, 27.0 us)
Async XLA Ops:
  7.2 244.3 %copy-start = (bf16[384,1536]{1,0:T(8,128)(2,1)S(1)}, bf16[384,1536]{1,0:T(8,128)(2,1)}, u32[]{:S(2)}) copy-start(bf16[384,1536]{1,0:T(8,128)(2,1)} %param.31) | copy-start | bytes 3538948
  7.2 82.1 %all-gather.8.cloned.1.call-start = ((), (), s32[]{:S(2)}) async-start(), calls=%async_computation.5 | async-start | bytes 1179648 | tf_op jit(solution)/shard_map/all_gather | solution.py:24
  8.8 2.7 copy-start.4
  8.8 2.7 copy-start.18
  8.9 3.5 %copy-start.16 = (f32[512]{0:T(512)}, f32[512]{0:T(512)S(1)}, u32[]{:S(2)}) copy-start(f32[512]{0:T(512)S(1)} %add_rsqrt_fusion.1) | copy-start | bytes 6148
  10.9 0.7 copy-start.9
  11.6 0.9 copy-start.10
  12.5 35.3 %copy-start.13 = (s32[128,1]{0,1:T(1,128)S(1)}, s32[128,1]{0,1:T(1,128)}, u32[]{:S(2)}) copy-start(s32[128,1]{0,1:T(1,128)} %param.21) | copy-start | bytes 1540
  45.2 38.1 %copy-start.5 = (bf16[512,1024]{1,0:T(8,128)(2,1)S(1)}, bf16[512,1024]{1,0:T(8,128)(2,1)}, u32[]{:S(2)}) copy-start(bf16[512,1024]{1,0:T(8,128)(2,1)} %param.19) | copy-start | bytes 3145732
  48.3 0.5 copy-start.14
  49.6 97.4 %all-to-all-start = ((s32[8,1,32]{2,1,0:T(1,128)}), s32[8,1,32]{2,1,0:T(1,128)}, u32[]{:S(2)}, u32[]{:S(2)}) async-start(s32[8,1,32]{2,1,0:T(1,128)} %select_n.96), calls=%async_computation | async-start | bytes 8192 | tf_op jit(solution)/shard_map/all_to_all | solution.py:192
  56.9 87.1 %all-reduce.3.cloned.1.call-start = ((), (), s32[]{:S(2)}) async-start(), calls=%async_computation.2 | async-start | bytes 2097152 | tf_op jit(solution)/shard_map/psum | solution.py:164
  103.8 1.7 copy-start.8
  105.9 1.2 copy-start.19
  107.2 1.8 copy-start.11
  107.2 1.9 copy-start.12
  109.2 36.4 %copy-start.15 = (s32[128]{0:T(128)S(1)}, s32[128]{0:T(128)}, u32[]{:S(2)}) copy-start(s32[128]{0:T(128)} %copy-done.14) | copy-start | bytes 1540
  145.6 21.0 %copy-start.1 = (bf16[512,1024]{1,0:T(8,128)(2,1)}, bf16[512,1024]{1,0:T(8,128)(2,1)S(1)}, u32[]{:S(2)}) copy-start(bf16[512,1024]{1,0:T(8,128)(2,1)S(1)} %fusion.47) | copy-start | bytes 3145732
  145.6 8.8 %copy-start.17 = (bf16[512]{0:T(512)(128)(2,1)S(1)}, bf16[512]{0:T(512)(128)(2,1)}, u32[]{:S(2)}) copy-start(bf16[512]{0:T(512)(128)(2,1)} %param.27) | copy-start | bytes 3076
  146.9 19.5 %all-to-all-start.1 = ((bf16[8,32,1024]{2,1,0:T(8,128)(2,1)}), bf16[8,32,1024]{2,1,0:T(8,128)(2,1)S(1)}, u32[]{:S(2)}, u32[]{:S(2)}) async-start(bf16[8,32,1024]{2,1,0:T(8,128)(2,1)} %bitcast.199), calls=%async_computation.1 | async-start | bytes 1048576 | tf_op jit(solution)/shard_map/all_to_all | solution.py:189
  152.4 82.2 %all-gather.6.cloned.1.call-start = ((), (), s32[]{:S(2)}) async-start(), calls=%async_computation.3 | async-start | bytes 1769472 | tf_op jit(solution)/shard_map/all_gather | solution.py:248
  154.5 59.3 %copy-start.6 = (bf16[256,512]{1,0:T(8,128)(2,1)}, bf16[256,512]{1,0:T(8,128)(2,1)S(1)}, u32[]{:S(2)}) copy-start(bf16[256,512]{1,0:T(8,128)(2,1)S(1)} %broadcast_select_fusion) | copy-start | bytes 786436
  166.4 47.5 %copy-start.2 = (bf16[8,32,1024]{2,1,0:T(8,128)(2,1)}, bf16[8,32,1024]{2,1,0:T(8,128)(2,1)S(1)}, u32[]{:S(2)}) copy-start(bf16[8,32,1024]{2,1,0:T(8,128)(2,1)S(1)} %all-to-all-done.1) | copy-start | bytes 1572868
  169.4 120.1 %all-reduce.5.cloned.1.call-start = ((), (), s32[]{:S(2)}) async-start(), calls=%async_computation.4 | async-start | bytes 1572864 | tf_op jit(solution)/shard_map/psum | solution.py:257
  171.7 8.5 %collective-permute-start = (bf16[256,3,128]{0,2,1:T(8,128)(2,1)S(1)}, bf16[256,3,128]{0,2,1:T(8,128)(2,1)S(1)}, u32[]{:S(2)}, u32[]{:S(2)}) collective-permute-start(bf16[256,3,128]{0,2,1:T(8,128)(2,1)S(1)} %bitcast.202), channel_id=1, source_target_pairs={{0,4},{4,8},{8,12},{12,16},{16,20},{20,24},{24,28},{28,0},{1,5},{5... | collective-permute-start | bytes 589832 | tf_op jit(solution)/shard_map/ppermute | solution.py:232
  180.2 10.4 %collective-permute-start.1 = (bf16[256,3,128]{0,2,1:T(8,128)(2,1)S(1)}, bf16[256,3,128]{0,2,1:T(8,128)(2,1)S(1)}, u32[]{:S(2)}, u32[]{:S(2)}) collective-permute-start(bf16[256,3,128]{0,2,1:T(8,128)(2,1)S(1)} %collective-permute-done), channel_id=1, source_target_pairs={{0,4},{4,8},{8,12},{12,16},{16,20},{20,24},{24,28},{28,0},{1,5},{5... | collective-permute-start | bytes 589832 | tf_op jit(solution)/shard_map/ppermute | solution.py:232
  180.2 31.6 %collective-permute-start.4 = (bf16[256,3,128]{0,2,1:T(8,128)(2,1)S(1)}, bf16[256,3,128]{0,2,1:T(8,128)(2,1)S(1)}, u32[]{:S(2)}, u32[]{:S(2)}) collective-permute-start(bf16[256,3,128]{0,2,1:T(8,128)(2,1)S(1)} %bitcast.203), channel_id=1, source_target_pairs={{4,0},{8,4},{12,8},{16,12},{20,16},{24,20},{28,24},{0,28},{5,1},{9... | collective-permute-start | bytes 589832 | tf_op jit(solution)/shard_map/ppermute | solution.py:234
  190.6 21.4 %collective-permute-start.2 = (bf16[256,3,128]{0,2,1:T(8,128)(2,1)S(1)}, bf16[256,3,128]{0,2,1:T(8,128)(2,1)S(1)}, u32[]{:S(2)}, u32[]{:S(2)}) collective-permute-start(bf16[256,3,128]{0,2,1:T(8,128)(2,1)S(1)} %collective-permute-done.1), channel_id=1, source_target_pairs={{0,4},{4,8},{8,12},{12,16},{16,20},{20,24},{24,28},{28,0},{1,5},{5... | collective-permute-start | bytes 589832 | tf_op jit(solution)/shard_map/ppermute | solution.py:232
  211.8 11.9 %collective-permute-start.5 = (bf16[256,3,128]{0,2,1:T(8,128)(2,1)S(1)}, bf16[256,3,128]{0,2,1:T(8,128)(2,1)}, u32[]{:S(2)}, u32[]{:S(2)}) collective-permute-start(bf16[256,3,128]{0,2,1:T(8,128)(2,1)S(1)} %collective-permute-done.4), channel_id=1, source_target_pairs={{4,0},{8,4},{12,8},{16,12},{20,16},{24,20},{28,24},{0,28},{5,1},{9... | collective-permute-start | bytes 589832 | tf_op jit(solution)/shard_map/ppermute | solution.py:234
  212.0 11.7 %collective-permute-start.3 = (bf16[256,3,128]{0,2,1:T(8,128)(2,1)S(1)}, bf16[256,3,128]{0,2,1:T(8,128)(2,1)}, u32[]{:S(2)}, u32[]{:S(2)}) collective-permute-start(bf16[256,3,128]{0,2,1:T(8,128)(2,1)S(1)} %collective-permute-done.2), channel_id=1, source_target_pairs={{0,4},{4,8},{8,12},{12,16},{16,20},{20,24},{24,28},{28,0},{1,5},{5... | collective-permute-start | bytes 589832 | tf_op jit(solution)/shard_map/ppermute | solution.py:232
  223.7 6.7 %collective-permute-start.6 = (bf16[256,3,128]{0,2,1:T(8,128)(2,1)}, bf16[256,3,128]{0,2,1:T(8,128)(2,1)S(1)}, u32[]{:S(2)}, u32[]{:S(2)}) collective-permute-start(bf16[256,3,128]{0,2,1:T(8,128)(2,1)} %collective-permute-done.5), channel_id=1, source_target_pairs={{4,0},{8,4},{12,8},{16,12},{20,16},{24,20},{28,24},{0,28},{5,1},{9... | collective-permute-start | bytes 589832 | tf_op jit(solution)/shard_map/ppermute | solution.py:234
  251.5 38.0 %copy-start.3 = (bf16[8,32,1024]{2,1,0:T(8,128)(2,1)S(1)}, bf16[8,32,1024]{2,1,0:T(8,128)(2,1)}, u32[]{:S(2)}) copy-start(bf16[8,32,1024]{2,1,0:T(8,128)(2,1)} %copy-done.2) | copy-start | bytes 1572868
  251.5 38.0 %copy-start.7 = (bf16[256,512]{1,0:T(8,128)(2,1)S(1)}, bf16[256,512]{1,0:T(8,128)(2,1)}, u32[]{:S(2)}) copy-start(bf16[256,512]{1,0:T(8,128)(2,1)} %copy-done.6) | copy-start | bytes 786436
Sparse Core Ops, SparseCore 0:
  46.1 43.2 all-gather.7
  109.1 34.8 all-reduce.2
  169.5 60.5 all-gather.5
  253.1 36.2 all-reduce.4
